TPU v7x, 128 devices: a whole 4x4x4 slice. The times are simulated.
128 devices in a mesh: segment: 4 (over z), band: 32 (over x, y, core).
Axes of the slice: x: 4, y: 4, z: 4, core: 2. Of those that a mesh axis runs over, the one named last changes fastest.
Arguments:
- clip: bfloat16 [2, 128, 160, 128], P(None, 'band'), may hold values from -6 to 6
- caches: bfloat16 [4, 4, 2, 128, 160, 128], P('segment', None, None, 'band'), may hold values from -4 to 4
- weights: bfloat16 [4, 4, 9, 3, 128, 128], P('segment'), may hold values from -0.109375 to 0.109375
- biases: float32 [4, 4, 128], P('segment'), may hold values from -2 to 2
- section_layers: int32 [4], P('segment'), may hold values from 1 to 4, as said below
Outputs:
- section_out: bfloat16 [4, 2, 128, 160, 128], P('segment', None, 'band')
Inputs may be any that keep to these rules, and one draw needn't show every extreme that they name: `section_layers`: each section has 1 to 4 layers, and some section has exactly 4.
All inputs are finite; a program needn't handle non-finite values.
Results may differ from a plain program's by a relative error of at most 0.024.
Values may be sent and summed in bfloat16 or wider, within the bound.
A program may use at most 128 MiB of HBM per device.

v0:
```python
import jax
import jax.numpy as jnp
from jax import lax
from jax.sharding import PartitionSpec as P


def extended(cells, sides, width):
    for axis, dim in sides:
        count = lax.axis_size(axis)
        ends = count - 1
        head = lax.slice_in_dim(cells, 0, width, axis=dim)
        tail = lax.slice_in_dim(cells, cells.shape[dim] - width, cells.shape[dim], axis=dim)
        cells = jnp.concatenate(
            [
                lax.ppermute(tail, axis, [(i, (i + 1) % count) for i in range(ends)]),
                cells,
                lax.ppermute(head, axis, [((i + 1) % count, i) for i in range(ends)]),
            ],
            axis=dim,
        )
    return cells


def shifted(value, axis, steps):
    count = lax.axis_size(axis)
    leading, last = (max(0, -steps), min(count, count - steps))
    return lax.ppermute(value, axis, [(source, source + steps) for source in range(leading, last)])


def conv_sum(padded, kernel, rows, width):
    channels = kernel.shape[-1]
    moved = jnp.transpose(padded, (1, 2, 0, 3))
    pieces = []
    for k in range(9):
        row_tap = k // 3
        col_tap = k % 3
        pieces.append(moved[row_tap : row_tap + rows, col_tap : col_tap + width])
    patches = jnp.stack(pieces, axis=2).reshape(rows * width, 27 * padded.shape[-1])
    flat_kernel = kernel.reshape(27 * kernel.shape[-2], channels)
    total = jnp.dot(patches, flat_kernel, preferred_element_type=jnp.float32)
    return total.reshape(rows, width, channels)


def per_device(clip, caches, weights, biases, section_layers):
    segment_count = lax.axis_size("segment")
    segment = lax.axis_index("segment")
    frames = clip.shape[0]
    rows = clip.shape[1]
    width = clip.shape[2]
    layer_total = weights.shape[1]
    count = section_layers[0]
    kernels = weights[0]
    bias_rows = biases[0]
    history = caches[0]
    received = jnp.zeros(clip.shape[1:], jnp.bfloat16)
    produced = jnp.zeros(clip.shape, jnp.bfloat16)
    frame_ids = jnp.arange(frames)
    ticks = frames + segment_count - 1
    for tick in range(ticks):
        frame = tick - segment
        valid = jnp.logical_and(frame >= 0, frame < frames)
        x_start = jnp.where(segment == 0, clip[min(tick, frames - 1)], received)

        def layer_step(layer, carry):
            x_now, hist = carry
            live = layer < count
            act = jax.nn.silu(x_now.astype(jnp.float32)).astype(jnp.bfloat16)
            kernel = lax.dynamic_index_in_dim(kernels, layer, 0, keepdims=False)
            past = lax.dynamic_index_in_dim(hist, layer, 0, keepdims=False)
            stack = jnp.concatenate([past, act[None]], axis=0)
            padded = extended(stack, (("band", 1),), 1)
            renewed = jnp.concatenate([past[1:], act[None]], axis=0)
            padded = jnp.pad(padded, ((0, 0), (0, 0), (1, 1), (0, 0)))
            total = conv_sum(padded, kernel, rows, width)
            bias = lax.dynamic_index_in_dim(bias_rows, layer, 0, keepdims=False)
            result = (x_now.astype(jnp.float32) + total + bias).astype(jnp.bfloat16)
            renewed = jnp.where(jnp.logical_and(valid, live), renewed, past)
            hist = lax.dynamic_update_index_in_dim(hist, renewed, layer, 0)
            return (jnp.where(live, result, x_now), hist)

        x_out, history = lax.fori_loop(0, layer_total, layer_step, (x_start, history))
        chosen = jnp.logical_and(valid, frame_ids == frame)
        produced = jnp.where(chosen[:, None, None, None], x_out[None], produced)
        if tick + 1 < ticks:
            received = shifted(x_out, "segment", 1)
    return produced[None]


def solution(mesh):
    placed = (
        P(None, "band", None, None),
        P("segment", None, None, "band", None, None),
        P("segment", None, None, None, None, None),
        P("segment", None, None),
        P("segment"),
    )
    return jax.shard_map(
        per_device,
        mesh=mesh,
        in_specs=placed,
        out_specs=P("segment", None, "band", None, None),
        check_vma=False,
    )
```

profile of v0, /device:TPU:102, one launch (start us, length us, event | category | flops | bytes accessed | tf_op | source)
XLA Modules:
  0.0 727.2 jit_solution(18349327235251145438)
XLA Ops:
  2.3 138.3 %while.85 = (s32[]{:T(128)}, bf16[4,160,128]{2,1,0:T(8,128)(2,1)S(1)}, bf16[4,2,4,160,128]{4,3,2,1,0:T(8,128)(2,1)S(1)}, s32[]{:T(128)}, bf16[4,9,3,128,128]{4,3...) while((s32[]{:T(128)}, bf16[4,160,128]{2,1,0:T(8,128)(2,1)S(1)}, ...), condition=%wide.region_1.2_spmd, body=%wide.region_0.1_spmd.sunk | while | flops 573672960 | bytes 39283432 | solution.py:81
  3.2 4.6 collective-permute-start
  11.7 4.5 collective-permute-done.1
  17.6 6.3 copy.61
  23.9 11.2 %dot_general.40 = bf16[4,160,3456]{2,1,0:T(8,128)(2,1)} reshape(bf16[4,160,9,3,128]{4,3,2,1,0:T(4,128)(2,1)} %copy.61) | data formatting | bytes 8847360 | tf_op jit(solution)/shard_map/while/body/eval_jaxpr/dot_general | solution.py:40
  46.1 4.0 collective-permute-done.1
  51.5 6.3 copy.61
  57.8 11.2 %dot_general.40 = bf16[4,160,3456]{2,1,0:T(8,128)(2,1)} reshape(bf16[4,160,9,3,128]{4,3,2,1,0:T(4,128)(2,1)} %copy.61) | data formatting | bytes 8847360 | tf_op jit(solution)/shard_map/while/body/eval_jaxpr/dot_general | solution.py:40
  80.0 4.0 collective-permute-done.1
  85.4 6.3 copy.61
  91.7 11.2 %dot_general.40 = bf16[4,160,3456]{2,1,0:T(8,128)(2,1)} reshape(bf16[4,160,9,3,128]{4,3,2,1,0:T(4,128)(2,1)} %copy.61) | data formatting | bytes 8847360 | tf_op jit(solution)/shard_map/while/body/eval_jaxpr/dot_general | solution.py:40
  113.9 4.0 collective-permute-done.1
  119.3 6.3 copy.61
  125.6 11.2 %dot_general.40 = bf16[4,160,3456]{2,1,0:T(8,128)(2,1)} reshape(bf16[4,160,9,3,128]{4,3,2,1,0:T(4,128)(2,1)} %copy.61) | data formatting | bytes 8847360 | tf_op jit(solution)/shard_map/while/body/eval_jaxpr/dot_general | solution.py:40
  142.4 5.4 collective-permute-done.10
  148.7 135.6 %while.86 = (s32[]{:T(128)}, bf16[4,160,128]{2,1,0:T(8,128)(2,1)S(1)}, bf16[4,2,4,160,128]{4,3,2,1,0:T(8,128)(2,1)S(1)}, s32[]{:T(128)}, bf16[4,9,3,128,128]{4,3...) while((s32[]{:T(128)}, bf16[4,160,128]{2,1,0:T(8,128)(2,1)S(1)}, ...), condition=%wide.region_3.4_spmd, body=%wide.region_2.3_spmd.sunk | while | flops 573672960 | bytes 39283432 | solution.py:81
  156.0 4.0 collective-permute-done.3
  161.3 6.3 copy.62
  167.7 11.2 %dot_general.41 = bf16[4,160,3456]{2,1,0:T(8,128)(2,1)} reshape(bf16[4,160,9,3,128]{4,3,2,1,0:T(4,128)(2,1)} %copy.62) | data formatting | bytes 8847360 | tf_op jit(solution)/shard_map/while/body/eval_jaxpr/dot_general | solution.py:40
  189.9 4.0 collective-permute-done.3
  195.2 6.3 copy.62
  201.6 11.2 %dot_general.41 = bf16[4,160,3456]{2,1,0:T(8,128)(2,1)} reshape(bf16[4,160,9,3,128]{4,3,2,1,0:T(4,128)(2,1)} %copy.62) | data formatting | bytes 8847360 | tf_op jit(solution)/shard_map/while/body/eval_jaxpr/dot_general | solution.py:40
  223.8 4.0 collective-permute-done.3
  229.1 6.3 copy.62
  235.5 11.2 %dot_general.41 = bf16[4,160,3456]{2,1,0:T(8,128)(2,1)} reshape(bf16[4,160,9,3,128]{4,3,2,1,0:T(4,128)(2,1)} %copy.62) | data formatting | bytes 8847360 | tf_op jit(solution)/shard_map/while/body/eval_jaxpr/dot_general | solution.py:40
  257.7 4.0 collective-permute-done.3
  263.0 6.3 copy.62
  269.4 11.2 %dot_general.41 = bf16[4,160,3456]{2,1,0:T(8,128)(2,1)} reshape(bf16[4,160,9,3,128]{4,3,2,1,0:T(4,128)(2,1)} %copy.62) | data formatting | bytes 8847360 | tf_op jit(solution)/shard_map/while/body/eval_jaxpr/dot_general | solution.py:40
  285.9 5.7 collective-permute-done.11
  292.5 135.6 %while.87 = (s32[]{:T(128)}, bf16[4,160,128]{2,1,0:T(8,128)(2,1)S(1)}, bf16[4,2,4,160,128]{4,3,2,1,0:T(8,128)(2,1)S(1)}, s32[]{:T(128)}, bf16[4,9,3,128,128]{4,3...) while((s32[]{:T(128)}, bf16[4,160,128]{2,1,0:T(8,128)(2,1)S(1)}, ...), condition=%wide.region_5.6_spmd, body=%wide.region_4.5_spmd.sunk | while | flops 573672960 | bytes 39283432 | solution.py:81
  299.8 4.0 collective-permute-done.5
  305.1 6.3 copy.63
  311.5 11.2 %dot_general.42 = bf16[4,160,3456]{2,1,0:T(8,128)(2,1)} reshape(bf16[4,160,9,3,128]{4,3,2,1,0:T(4,128)(2,1)} %copy.63) | data formatting | bytes 8847360 | tf_op jit(solution)/shard_map/while/body/eval_jaxpr/dot_general | solution.py:40
  333.7 4.0 collective-permute-done.5
  339.0 6.3 copy.63
  345.4 11.2 %dot_general.42 = bf16[4,160,3456]{2,1,0:T(8,128)(2,1)} reshape(bf16[4,160,9,3,128]{4,3,2,1,0:T(4,128)(2,1)} %copy.63) | data formatting | bytes 8847360 | tf_op jit(solution)/shard_map/while/body/eval_jaxpr/dot_general | solution.py:40
  372.9 6.3 copy.63
  379.3 11.2 %dot_general.42 = bf16[4,160,3456]{2,1,0:T(8,128)(2,1)} reshape(bf16[4,160,9,3,128]{4,3,2,1,0:T(4,128)(2,1)} %copy.63) | data formatting | bytes 8847360 | tf_op jit(solution)/shard_map/while/body/eval_jaxpr/dot_general | solution.py:40
  406.8 6.3 copy.63
  413.2 11.2 %dot_general.42 = bf16[4,160,3456]{2,1,0:T(8,128)(2,1)} reshape(bf16[4,160,9,3,128]{4,3,2,1,0:T(4,128)(2,1)} %copy.63) | data formatting | bytes 8847360 | tf_op jit(solution)/shard_map/while/body/eval_jaxpr/dot_general | solution.py:40
  429.7 5.7 collective-permute-done.12
  436.3 138.1 %while.88 = (s32[]{:T(128)}, bf16[4,160,128]{2,1,0:T(8,128)(2,1)S(1)}, bf16[4,2,4,160,128]{4,3,2,1,0:T(8,128)(2,1)S(1)}, s32[]{:T(128)}, bf16[4,9,3,128,128]{4,3...) while((s32[]{:T(128)}, bf16[4,160,128]{2,1,0:T(8,128)(2,1)S(1)}, ...), condition=%wide.region_7.8_spmd, body=%wide.region_6.7_spmd.sunk | while | flops 573672960 | bytes 39283432 | solution.py:81
  449.5 6.3 copy.64
  455.8 11.2 %dot_general.43 = bf16[4,160,3456]{2,1,0:T(8,128)(2,1)} reshape(bf16[4,160,9,3,128]{4,3,2,1,0:T(4,128)(2,1)} %copy.64) | data formatting | bytes 8847360 | tf_op jit(solution)/shard_map/while/body/eval_jaxpr/dot_general | solution.py:40
  484.0 6.3 copy.64
  490.4 11.2 %dot_general.43 = bf16[4,160,3456]{2,1,0:T(8,128)(2,1)} reshape(bf16[4,160,9,3,128]{4,3,2,1,0:T(4,128)(2,1)} %copy.64) | data formatting | bytes 8847360 | tf_op jit(solution)/shard_map/while/body/eval_jaxpr/dot_general | solution.py:40
  518.5 6.3 copy.64
  524.9 11.2 %dot_general.43 = bf16[4,160,3456]{2,1,0:T(8,128)(2,1)} reshape(bf16[4,160,9,3,128]{4,3,2,1,0:T(4,128)(2,1)} %copy.64) | data formatting | bytes 8847360 | tf_op jit(solution)/shard_map/while/body/eval_jaxpr/dot_general | solution.py:40
  553.1 6.3 copy.64
  559.4 11.2 %dot_general.43 = bf16[4,160,3456]{2,1,0:T(8,128)(2,1)} reshape(bf16[4,160,9,3,128]{4,3,2,1,0:T(4,128)(2,1)} %copy.64) | data formatting | bytes 8847360 | tf_op jit(solution)/shard_map/while/body/eval_jaxpr/dot_general | solution.py:40
  576.0 5.6 collective-permute-done.13
  582.6 143.5 %while.89 = (s32[]{:T(128)}, bf16[4,160,128]{2,1,0:T(8,128)(2,1)S(1)}, bf16[4,2,4,160,128]{4,3,2,1,0:T(8,128)(2,1)S(1)}, s32[]{:T(128)}, bf16[4,9,3,128,128]{4,3...) while((s32[]{:T(128)}, bf16[4,160,128]{2,1,0:T(8,128)(2,1)S(1)}, ...), condition=%wide.region_9.10_spmd, body=%wide.region_8.9_spmd.sunk | while | flops 573672960 | bytes 39283432 | solution.py:81
  590.5 4.3 collective-permute-done.9
  597.1 6.3 copy.65
  603.5 11.2 %dot_general.44 = bf16[4,160,3456]{2,1,0:T(8,128)(2,1)} reshape(bf16[4,160,9,3,128]{4,3,2,1,0:T(4,128)(2,1)} %copy.65) | data formatting | bytes 8847360 | tf_op jit(solution)/shard_map/while/body/eval_jaxpr/dot_general | solution.py:40
  626.4 4.3 collective-permute-done.9
  633.0 6.3 copy.65
  639.3 11.2 %dot_general.44 = bf16[4,160,3456]{2,1,0:T(8,128)(2,1)} reshape(bf16[4,160,9,3,128]{4,3,2,1,0:T(4,128)(2,1)} %copy.65) | data formatting | bytes 8847360 | tf_op jit(solution)/shard_map/while/body/eval_jaxpr/dot_general | solution.py:40
  662.2 4.3 collective-permute-done.9
  668.9 6.3 copy.65
  675.2 11.2 %dot_general.44 = bf16[4,160,3456]{2,1,0:T(8,128)(2,1)} reshape(bf16[4,160,9,3,128]{4,3,2,1,0:T(4,128)(2,1)} %copy.65) | data formatting | bytes 8847360 | tf_op jit(solution)/shard_map/while/body/eval_jaxpr/dot_general | solution.py:40
  698.1 4.3 collective-permute-done.9
  704.7 6.3 copy.65
  711.0 11.2 %dot_general.44 = bf16[4,160,3456]{2,1,0:T(8,128)(2,1)} reshape(bf16[4,160,9,3,128]{4,3,2,1,0:T(4,128)(2,1)} %copy.65) | data formatting | bytes 8847360 | tf_op jit(solution)/shard_map/while/body/eval_jaxpr/dot_general | solution.py:40
  (427 shorter events, 275.8 us)
Async XLA Ops:
  3.2 8.5 %collective-permute-start = (bf16[3,1,160,128]{3,2,1,0:T(8,128)(2,1)S(1)}, bf16[3,1,160,128]{3,2,1,0:T(8,128)(2,1)S(1)}, u32[]{:S(2)}, u32[]{:S(2)}) collective-permute-start(bf16[3,1,160,128]{3,2,1,0:T(8,128)(2,1)S(1)} %get-tuple-element.1222), channel_id=1, source_target_pairs={{1,0},{2,1},{3,2},{4,3},{5,4},{6,5},{7,6},{8,7},{9,8},{10,9},{11,1... | collective-permute-start | bytes 368648 | tf_op jit(solution)/shard_map/while/body/eval_jaxpr/ppermute | solution.py:17
  7.9 8.3 %collective-permute-start.1 = (bf16[3,1,160,128]{3,2,1,0:T(8,128)(2,1)S(1)}, bf16[3,1,160,128]{3,2,1,0:T(8,128)(2,1)S(1)}, u32[]{:S(2)}, u32[]{:S(2)}) collective-permute-start(bf16[3,1,160,128]{3,2,1,0:T(8,128)(2,1)S(1)} %get-tuple-element.1223), channel_id=1, source_target_pairs={{0,1},{1,2},{2,3},{3,4},{4,5},{5,6},{6,7},{7,8},{8,9},{9,10},{10,1... | collective-permute-start | bytes 368648 | tf_op jit(solution)/shard_map/while/body/eval_jaxpr/ppermute | solution.py:15
  39.8 6.3 collective-permute-start
  41.8 8.3 %collective-permute-start.1 = (bf16[3,1,160,128]{3,2,1,0:T(8,128)(2,1)S(1)}, bf16[3,1,160,128]{3,2,1,0:T(8,128)(2,1)S(1)}, u32[]{:S(2)}, u32[]{:S(2)}) collective-permute-start(bf16[3,1,160,128]{3,2,1,0:T(8,128)(2,1)S(1)} %get-tuple-element.1223), channel_id=1, source_target_pairs={{0,1},{1,2},{2,3},{3,4},{4,5},{5,6},{6,7},{7,8},{8,9},{9,10},{10,1... | collective-permute-start | bytes 368648 | tf_op jit(solution)/shard_map/while/body/eval_jaxpr/ppermute | solution.py:15
  73.7 6.3 collective-permute-start
  75.7 8.3 %collective-permute-start.1 = (bf16[3,1,160,128]{3,2,1,0:T(8,128)(2,1)S(1)}, bf16[3,1,160,128]{3,2,1,0:T(8,128)(2,1)S(1)}, u32[]{:S(2)}, u32[]{:S(2)}) collective-permute-start(bf16[3,1,160,128]{3,2,1,0:T(8,128)(2,1)S(1)} %get-tuple-element.1223), channel_id=1, source_target_pairs={{0,1},{1,2},{2,3},{3,4},{4,5},{5,6},{6,7},{7,8},{8,9},{9,10},{10,1... | collective-permute-start | bytes 368648 | tf_op jit(solution)/shard_map/while/body/eval_jaxpr/ppermute | solution.py:15
  107.7 6.3 collective-permute-start
  109.6 8.3 %collective-permute-start.1 = (bf16[3,1,160,128]{3,2,1,0:T(8,128)(2,1)S(1)}, bf16[3,1,160,128]{3,2,1,0:T(8,128)(2,1)S(1)}, u32[]{:S(2)}, u32[]{:S(2)}) collective-permute-start(bf16[3,1,160,128]{3,2,1,0:T(8,128)(2,1)S(1)} %get-tuple-element.1223), channel_id=1, source_target_pairs={{0,1},{1,2},{2,3},{3,4},{4,5},{5,6},{6,7},{7,8},{8,9},{9,10},{10,1... | collective-permute-start | bytes 368648 | tf_op jit(solution)/shard_map/while/body/eval_jaxpr/ppermute | solution.py:15
  140.6 1.8 copy-start.2
  140.6 7.2 collective-permute-start.10
  149.7 6.3 collective-permute-start.2
  151.7 8.3 %collective-permute-start.3 = (bf16[3,1,160,128]{3,2,1,0:T(8,128)(2,1)S(1)}, bf16[3,1,160,128]{3,2,1,0:T(8,128)(2,1)S(1)}, u32[]{:S(2)}, u32[]{:S(2)}) collective-permute-start(bf16[3,1,160,128]{3,2,1,0:T(8,128)(2,1)S(1)} %get-tuple-element.1236), channel_id=1, source_target_pairs={{0,1},{1,2},{2,3},{3,4},{4,5},{5,6},{6,7},{7,8},{8,9},{9,10},{10,1... | collective-permute-start | bytes 368648 | tf_op jit(solution)/shard_map/while/body/eval_jaxpr/ppermute | solution.py:15
  183.6 6.3 collective-permute-start.2
  185.6 8.3 %collective-permute-start.3 = (bf16[3,1,160,128]{3,2,1,0:T(8,128)(2,1)S(1)}, bf16[3,1,160,128]{3,2,1,0:T(8,128)(2,1)S(1)}, u32[]{:S(2)}, u32[]{:S(2)}) collective-permute-start(bf16[3,1,160,128]{3,2,1,0:T(8,128)(2,1)S(1)} %get-tuple-element.1236), channel_id=1, source_target_pairs={{0,1},{1,2},{2,3},{3,4},{4,5},{5,6},{6,7},{7,8},{8,9},{9,10},{10,1... | collective-permute-start | bytes 368648 | tf_op jit(solution)/shard_map/while/body/eval_jaxpr/ppermute | solution.py:15
  217.5 6.3 collective-permute-start.2
  219.5 8.3 %collective-permute-start.3 = (bf16[3,1,160,128]{3,2,1,0:T(8,128)(2,1)S(1)}, bf16[3,1,160,128]{3,2,1,0:T(8,128)(2,1)S(1)}, u32[]{:S(2)}, u32[]{:S(2)}) collective-permute-start(bf16[3,1,160,128]{3,2,1,0:T(8,128)(2,1)S(1)} %get-tuple-element.1236), channel_id=1, source_target_pairs={{0,1},{1,2},{2,3},{3,4},{4,5},{5,6},{6,7},{7,8},{8,9},{9,10},{10,1... | collective-permute-start | bytes 368648 | tf_op jit(solution)/shard_map/while/body/eval_jaxpr/ppermute | solution.py:15
  251.4 6.3 collective-permute-start.2
  253.4 8.3 %collective-permute-start.3 = (bf16[3,1,160,128]{3,2,1,0:T(8,128)(2,1)S(1)}, bf16[3,1,160,128]{3,2,1,0:T(8,128)(2,1)S(1)}, u32[]{:S(2)}, u32[]{:S(2)}) collective-permute-start(bf16[3,1,160,128]{3,2,1,0:T(8,128)(2,1)S(1)} %get-tuple-element.1236), channel_id=1, source_target_pairs={{0,1},{1,2},{2,3},{3,4},{4,5},{5,6},{6,7},{7,8},{8,9},{9,10},{10,1... | collective-permute-start | bytes 368648 | tf_op jit(solution)/shard_map/while/body/eval_jaxpr/ppermute | solution.py:15
  284.4 8.2 %copy-start = (bf16[4,160,128]{2,1,0:T(8,128)(2,1)}, bf16[4,160,128]{2,1,0:T(8,128)(2,1)S(1)}, u32[]{:S(2)}) copy-start(bf16[4,160,128]{2,1,0:T(8,128)(2,1)S(1)} %get-tuple-element.891) | copy-start | bytes 491524
  284.4 7.2 collective-permute-start.11
  293.5 6.3 collective-permute-start.4
  295.4 8.3 %collective-permute-start.5 = (bf16[3,1,160,128]{3,2,1,0:T(8,128)(2,1)S(1)}, bf16[3,1,160,128]{3,2,1,0:T(8,128)(2,1)S(1)}, u32[]{:S(2)}, u32[]{:S(2)}) collective-permute-start(bf16[3,1,160,128]{3,2,1,0:T(8,128)(2,1)S(1)} %get-tuple-element.1249), channel_id=1, source_target_pairs={{0,1},{1,2},{2,3},{3,4},{4,5},{5,6},{6,7},{7,8},{8,9},{9,10},{10,1... | collective-permute-start | bytes 368648 | tf_op jit(solution)/shard_map/while/body/eval_jaxpr/ppermute | solution.py:15
  327.4 6.3 collective-permute-start.4
  329.3 8.3 %collective-permute-start.5 = (bf16[3,1,160,128]{3,2,1,0:T(8,128)(2,1)S(1)}, bf16[3,1,160,128]{3,2,1,0:T(8,128)(2,1)S(1)}, u32[]{:S(2)}, u32[]{:S(2)}) collective-permute-start(bf16[3,1,160,128]{3,2,1,0:T(8,128)(2,1)S(1)} %get-tuple-element.1249), channel_id=1, source_target_pairs={{0,1},{1,2},{2,3},{3,4},{4,5},{5,6},{6,7},{7,8},{8,9},{9,10},{10,1... | collective-permute-start | bytes 368648 | tf_op jit(solution)/shard_map/while/body/eval_jaxpr/ppermute | solution.py:15
  361.3 6.3 collective-permute-start.4
  363.2 8.3 %collective-permute-start.5 = (bf16[3,1,160,128]{3,2,1,0:T(8,128)(2,1)S(1)}, bf16[3,1,160,128]{3,2,1,0:T(8,128)(2,1)S(1)}, u32[]{:S(2)}, u32[]{:S(2)}) collective-permute-start(bf16[3,1,160,128]{3,2,1,0:T(8,128)(2,1)S(1)} %get-tuple-element.1249), channel_id=1, source_target_pairs={{0,1},{1,2},{2,3},{3,4},{4,5},{5,6},{6,7},{7,8},{8,9},{9,10},{10,1... | collective-permute-start | bytes 368648 | tf_op jit(solution)/shard_map/while/body/eval_jaxpr/ppermute | solution.py:15
  395.2 6.3 collective-permute-start.4
  397.2 8.3 %collective-permute-start.5 = (bf16[3,1,160,128]{3,2,1,0:T(8,128)(2,1)S(1)}, bf16[3,1,160,128]{3,2,1,0:T(8,128)(2,1)S(1)}, u32[]{:S(2)}, u32[]{:S(2)}) collective-permute-start(bf16[3,1,160,128]{3,2,1,0:T(8,128)(2,1)S(1)} %get-tuple-element.1249), channel_id=1, source_target_pairs={{0,1},{1,2},{2,3},{3,4},{4,5},{5,6},{6,7},{7,8},{8,9},{9,10},{10,1... | collective-permute-start | bytes 368648 | tf_op jit(solution)/shard_map/while/body/eval_jaxpr/ppermute | solution.py:15
  428.1 7.2 collective-permute-start.12
  437.9 6.3 collective-permute-start.6
  439.8 8.3 %collective-permute-start.7 = (bf16[3,1,160,128]{3,2,1,0:T(8,128)(2,1)S(1)}, bf16[3,1,160,128]{3,2,1,0:T(8,128)(2,1)S(1)}, u32[]{:S(2)}, u32[]{:S(2)}) collective-permute-start(bf16[3,1,160,128]{3,2,1,0:T(8,128)(2,1)S(1)} %get-tuple-element.1262), channel_id=1, source_target_pairs={{0,1},{1,2},{2,3},{3,4},{4,5},{5,6},{6,7},{7,8},{8,9},{9,10},{10,1... | collective-permute-start | bytes 368648 | tf_op jit(solution)/shard_map/while/body/eval_jaxpr/ppermute | solution.py:15
  472.4 6.3 collective-permute-start.6
  474.3 8.3 %collective-permute-start.7 = (bf16[3,1,160,128]{3,2,1,0:T(8,128)(2,1)S(1)}, bf16[3,1,160,128]{3,2,1,0:T(8,128)(2,1)S(1)}, u32[]{:S(2)}, u32[]{:S(2)}) collective-permute-start(bf16[3,1,160,128]{3,2,1,0:T(8,128)(2,1)S(1)} %get-tuple-element.1262), channel_id=1, source_target_pairs={{0,1},{1,2},{2,3},{3,4},{4,5},{5,6},{6,7},{7,8},{8,9},{9,10},{10,1... | collective-permute-start | bytes 368648 | tf_op jit(solution)/shard_map/while/body/eval_jaxpr/ppermute | solution.py:15
  506.9 6.3 collective-permute-start.6
  508.9 8.3 %collective-permute-start.7 = (bf16[3,1,160,128]{3,2,1,0:T(8,128)(2,1)S(1)}, bf16[3,1,160,128]{3,2,1,0:T(8,128)(2,1)S(1)}, u32[]{:S(2)}, u32[]{:S(2)}) collective-permute-start(bf16[3,1,160,128]{3,2,1,0:T(8,128)(2,1)S(1)} %get-tuple-element.1262), channel_id=1, source_target_pairs={{0,1},{1,2},{2,3},{3,4},{4,5},{5,6},{6,7},{7,8},{8,9},{9,10},{10,1... | collective-permute-start | bytes 368648 | tf_op jit(solution)/shard_map/while/body/eval_jaxpr/ppermute | solution.py:15
  541.5 6.3 collective-permute-start.6
  543.4 8.3 %collective-permute-start.7 = (bf16[3,1,160,128]{3,2,1,0:T(8,128)(2,1)S(1)}, bf16[3,1,160,128]{3,2,1,0:T(8,128)(2,1)S(1)}, u32[]{:S(2)}, u32[]{:S(2)}) collective-permute-start(bf16[3,1,160,128]{3,2,1,0:T(8,128)(2,1)S(1)} %get-tuple-element.1262), channel_id=1, source_target_pairs={{0,1},{1,2},{2,3},{3,4},{4,5},{5,6},{6,7},{7,8},{8,9},{9,10},{10,1... | collective-permute-start | bytes 368648 | tf_op jit(solution)/shard_map/while/body/eval_jaxpr/ppermute | solution.py:15
  574.4 7.2 collective-permute-start.13
  582.5 143.5 %copy-start.1 = (bf16[4,160,128]{2,1,0:T(8,128)(2,1)S(1)}, bf16[4,160,128]{2,1,0:T(8,128)(2,1)}, u32[]{:S(2)}) copy-start(bf16[4,160,128]{2,1,0:T(8,128)(2,1)} %copy-done) | copy-start | bytes 491524
  582.5 143.5 %copy-start.3 = (bf16[4,160,128]{2,1,0:T(8,128)(2,1)S(1)}, bf16[4,160,128]{2,1,0:T(8,128)(2,1)}, u32[]{:S(2)}) copy-start(bf16[4,160,128]{2,1,0:T(8,128)(2,1)} %copy-done.2) | copy-start | bytes 491524
  584.3 6.3 collective-permute-start.8
  586.2 8.6 %collective-permute-start.9 = (bf16[3,1,160,128]{3,2,1,0:T(8,128)(2,1)}, bf16[3,1,160,128]{3,2,1,0:T(8,128)(2,1)}, u32[]{:S(2)}, u32[]{:S(2)}) collective-permute-start(bf16[3,1,160,128]{3,2,1,0:T(8,128)(2,1)} %get-tuple-element.1275), channel_id=1, source_target_pairs={{0,1},{1,2},{2,3},{3,4},{4,5},{5,6},{6,7},{7,8},{8,9},{9,10},{10,1... | collective-permute-start | bytes 368648 | tf_op jit(solution)/shard_map/while/body/eval_jaxpr/ppermute | solution.py:15
  620.1 6.3 collective-permute-start.8
  622.0 8.6 %collective-permute-start.9 = (bf16[3,1,160,128]{3,2,1,0:T(8,128)(2,1)}, bf16[3,1,160,128]{3,2,1,0:T(8,128)(2,1)}, u32[]{:S(2)}, u32[]{:S(2)}) collective-permute-start(bf16[3,1,160,128]{3,2,1,0:T(8,128)(2,1)} %get-tuple-element.1275), channel_id=1, source_target_pairs={{0,1},{1,2},{2,3},{3,4},{4,5},{5,6},{6,7},{7,8},{8,9},{9,10},{10,1... | collective-permute-start | bytes 368648 | tf_op jit(solution)/shard_map/while/body/eval_jaxpr/ppermute | solution.py:15
  656.0 6.3 collective-permute-start.8
  657.9 8.6 %collective-permute-start.9 = (bf16[3,1,160,128]{3,2,1,0:T(8,128)(2,1)}, bf16[3,1,160,128]{3,2,1,0:T(8,128)(2,1)}, u32[]{:S(2)}, u32[]{:S(2)}) collective-permute-start(bf16[3,1,160,128]{3,2,1,0:T(8,128)(2,1)} %get-tuple-element.1275), channel_id=1, source_target_pairs={{0,1},{1,2},{2,3},{3,4},{4,5},{5,6},{6,7},{7,8},{8,9},{9,10},{10,1... | collective-permute-start | bytes 368648 | tf_op jit(solution)/shard_map/while/body/eval_jaxpr/ppermute | solution.py:15
  691.8 6.3 collective-permute-start.8
  693.8 8.6 %collective-permute-start.9 = (bf16[3,1,160,128]{3,2,1,0:T(8,128)(2,1)}, bf16[3,1,160,128]{3,2,1,0:T(8,128)(2,1)}, u32[]{:S(2)}, u32[]{:S(2)}) collective-permute-start(bf16[3,1,160,128]{3,2,1,0:T(8,128)(2,1)} %get-tuple-element.1275), channel_id=1, source_target_pairs={{0,1},{1,2},{2,3},{3,4},{4,5},{5,6},{6,7},{7,8},{8,9},{9,10},{10,1... | collective-permute-start | bytes 368648 | tf_op jit(solution)/shard_map/while/body/eval_jaxpr/ppermute | solution.py:15
where the time goes:
time: 742 us; the launch traced here: 727 us
  local copies, waits for them, and re-layouts  414 us (56%)
  waiting for transfers between devices  104 us (14%)
  starting transfers between devices  95 us (13%)
  matrix products  74.7 us (10%)
  other arithmetic  24.5 us (3%)
  loops' own time  15.4 us (2%)
    dot_general x20, local copies, waits for them, and re-layouts, conv_sum(): total = jnp.dot(patches, flat_kernel, preferred_element_type=jnp.float32)  225 us
    another operation x40, local copies, waits for them, and re-layouts, conv_sum(): jnp.stack(pieces, axis=2).reshape(rows * width, 27 * padded.shape[-1])  130 us
    ppermute x20, waiting for transfers between devices, extended(): lax.ppermute(tail, axis, [(i, (i + 1) % count) for i in range(ends)])  81.1 us
    dot_general x20, matrix products, conv_sum(): total = jnp.dot(patches, flat_kernel, preferred_element_type=jnp.float32)  74.7 us
    ppermute x20, starting transfers between devices, extended(): lax.ppermute(tail, axis, [(i, (i + 1) % count) for i in range(ends)])  47.6 us
    ppermute x20, starting transfers between devices, extended(): lax.ppermute(head, axis, [((i + 1) % count, i) for i in range(ends)])  41 us
    dynamic_slice x20, local copies, waits for them, and re-layouts, layer_step(): kernel = lax.dynamic_index_in_dim(kernels, layer, 0, keepdims=False)  24.6 us
    ppermute x4, waiting for transfers between devices, shifted(): lax.ppermute(value, axis, [(source, source + steps) for source in range(l...  22.4 us
  transfers between devices with their start and end apart: 44, of which 24 were waited for; matrix products, arithmetic and copies ran while one was open for 5% of the time, Pallas kernels for 0%

commit v1 on v0

v1 whole, which is shorter than its diff:
```python
import functools

import jax
import jax.numpy as jnp
from jax import lax
from jax.experimental import pallas as pl
from jax.experimental.pallas import tpu as pltpu
from jax.sharding import PartitionSpec as P

MESH = pl.DeviceIdType.MESH
PAD = 8


def kernel(dims, live_ref, bias_ref, clip, caches, weights, out, *scratch):
    segments, bands, frames, own, width, chan, depth = dims
    (wd, cext, c3, a3, sh, xs, xin, outs) = scratch[:8]
    p0 = scratch[8 : 8 + depth]
    p1 = scratch[8 + depth : 8 + 2 * depth]
    (w_sem, cl_sem, ch_send, ch_recv, cm_sem, k_send, x_send, x_recv, out_sem) = scratch[8 + 2 * depth :]
    halo = depth
    ext = own + 2 * halo
    seg = lax.axis_index("segment")
    band = lax.axis_index("band")
    first, last = seg == 0, seg == segments - 1
    has_up, has_down = band > 0, band < bands - 1

    w_copies = [
        [
            pltpu.make_async_copy(
                weights.at[0, l, :, t],
                wd.at[l, :, :, pl.ds((2 - t) * chan, chan)],
                w_sem.at[l, t],
            )
            for t in range(3)
        ]
        for l in range(depth)
    ]
    cl_copies = [
        pltpu.make_async_copy(caches.at[0, l], cext.at[l, :, pl.ds(halo, own)], cl_sem.at[l])
        for l in range(depth)
    ]
    clip_copy = pltpu.make_async_copy(clip, xin.at[:, pl.ds(halo, own)], cm_sem)
    for l in range(depth):
        cl_copies[l].start()
        for t in range(3):
            w_copies[l][t].start()

    @pl.when(first)
    def _():
        clip_copy.start()

    barrier = pltpu.get_barrier_semaphore()
    up_n, down_n = has_up.astype(jnp.int32), has_down.astype(jnp.int32)
    before, after = 1 - first.astype(jnp.int32), 1 - last.astype(jnp.int32)

    def greet(cond, ds, db):
        @pl.when(cond)
        def _():
            pl.semaphore_signal(
                barrier, inc=1, device_id={"segment": seg + ds, "band": band + db}, device_id_type=MESH
            )

    greet(has_up, 0, -1)
    greet(has_down, 0, 1)
    for ds, cond in ((-1, jnp.logical_not(first)), (1, jnp.logical_not(last))):
        greet(cond, ds, 0)
        greet(jnp.logical_and(cond, has_up), ds, -1)
        greet(jnp.logical_and(cond, has_down), ds, 1)
    pl.semaphore_wait(barrier, (up_n + down_n) * (1 + before + after) + before + after)

    def cache_down(l):
        return pltpu.make_async_remote_copy(
            caches.at[0, l, :, pl.ds(l, own - l)],
            cext.at[l, :, pl.ds(l, own - l)],
            ch_send.at[l, 0],
            ch_recv.at[l, 0],
            device_id={"segment": seg, "band": band + 1},
            device_id_type=MESH,
        )

    def cache_up(l):
        return pltpu.make_async_remote_copy(
            caches.at[0, l, :, pl.ds(0, own - l)],
            cext.at[l, :, pl.ds(halo + own, own - l)],
            ch_send.at[l, 1],
            ch_recv.at[l, 1],
            device_id={"segment": seg, "band": band - 1},
            device_id_type=MESH,
        )

    def place(k):
        return (pl.ds(0, halo), pl.ds(halo, own), pl.ds(halo + own, halo))[k]

    def clip_send(f, k):
        return pltpu.make_async_remote_copy(
            clip.at[f],
            xin.at[f, place(k)],
            k_send.at[f, k // 2],
            x_recv.at[f, k],
            device_id={"segment": seg, "band": band + 1 - k},
            device_id_type=MESH,
        )

    def x_copy(f, k):
        return pltpu.make_async_remote_copy(
            outs.at[f],
            xin.at[f, place(k)],
            x_send.at[f, k],
            x_recv.at[f, k],
            device_id={"segment": seg + 1, "band": band + 1 - k},
            device_id_type=MESH,
        )

    def both(side, fn_list):
        @pl.when(side)
        def _():
            for fn in fn_list:
                fn()

    seg0_down, seg0_up = jnp.logical_and(first, has_down), jnp.logical_and(first, has_up)
    both(seg0_down, [lambda: clip_send(0, 0).start()])
    both(seg0_up, [lambda: clip_send(0, 2).start()])
    for l in range(depth):
        both(has_down, [lambda l=l: cache_down(l).start()])
        both(has_up, [lambda l=l: cache_up(l).start()])
    both(seg0_down, [lambda: clip_send(1, 0).start()])
    both(seg0_up, [lambda: clip_send(1, 2).start()])

    sh[:, 0:PAD, :] = jnp.zeros((sh.shape[0], PAD, chan), jnp.float32)
    sh[:, PAD + width : 2 * PAD + width, :] = jnp.zeros((sh.shape[0], PAD, chan), jnp.float32)

    @pl.when(jnp.logical_not(has_up))
    def _():
        cext[:, :, 0:halo] = jnp.zeros((depth, 2, halo, width, chan), jnp.bfloat16)
        xin[:, 0:halo] = jnp.zeros((frames, halo, width, chan), jnp.bfloat16)

    @pl.when(jnp.logical_not(has_down))
    def _():
        cext[:, :, halo + own :] = jnp.zeros((depth, 2, halo, width, chan), jnp.bfloat16)
        xin[:, halo + own :] = jnp.zeros((frames, halo, width, chan), jnp.bfloat16)

    def put_shifted(dst, row, value):
        sh[row, PAD : PAD + width, :] = value
        dst[row, :, 0:chan] = sh[row, PAD - 1 : PAD - 1 + width, :].astype(jnp.bfloat16)
        dst[row, :, chan : 2 * chan] = value.astype(jnp.bfloat16)
        dst[row, :, 2 * chan : 3 * chan] = sh[row, PAD + 1 : PAD + 1 + width, :].astype(jnp.bfloat16)

    def patches(src, row):
        parts = [src[pl.ds(row - 1 + i, 2)].reshape(2 * width, 3 * chan) for i in range(3)]
        return jnp.concatenate(parts, axis=1)

    def taps(l, lo, hi):
        return wd[l, :, :, lo * chan : hi * chan].reshape(9 * chan, (hi - lo) * chan)

    def dot(a, b):
        return jnp.dot(a, b, preferred_element_type=jnp.float32)

    for l in range(depth):
        for t in range(3):
            w_copies[l][t].wait()
        cl_copies[l].wait()
        both(has_up, [lambda l=l: cache_down(l).wait_recv()])
        both(has_down, [lambda l=l: cache_up(l).wait_recv()])

        def spread(row, carry, l=l):
            for f in range(2):
                put_shifted(c3.at[f], row, cext[l, f, row].astype(jnp.float32))
            return carry

        lax.fori_loop(l, ext - l, spread, 0)

        def past(q, carry, l=l):
            row = l + 1 + 2 * q
            newer = dot(patches(c3.at[1], row), taps(l, 1, 3))
            older = dot(patches(c3.at[0], row), taps(l, 2, 3))
            bias = bias_ref[l]
            p0[l][pl.ds(2 * q, 2)] = (newer[:, :chan] + older + bias).reshape(2, width, chan)
            p1[l][pl.ds(2 * q, 2)] = (newer[:, chan:] + bias).reshape(2, width, chan)
            return carry

        lax.fori_loop(0, (own + 2 * (halo - 1 - l)) // 2, past, 0)

    def activate(dst, row, x):
        at = band * own + row - halo
        inside = jnp.logical_and(at >= 0, at < bands * own)
        act = x * (0.5 * jnp.tanh(0.5 * x) + 0.5)
        put_shifted(dst, row, jnp.where(inside, act, 0.0))

    for f in range(frames):
        if f == 0:
            @pl.when(first)
            def _():
                clip_copy.wait()

        @pl.when(jnp.logical_not(first))
        def _(f=f):
            x_copy(f, 1).wait_recv()

        both(has_up, [lambda f=f: x_copy(f, 0).wait_recv()])
        both(has_down, [lambda f=f: x_copy(f, 2).wait_recv()])

        def enter(row, carry, f=f):
            x = xin[f, row].astype(jnp.float32)
            xs[row] = x
            activate(a3.at[0], row, x)
            return carry

        lax.fori_loop(0, ext, enter, 0)
        for l in range(depth):

            def layer(q, carry, f=f, l=l):
                row = l + 1 + 2 * q
                src, dst = a3.at[l % 2], a3.at[(l + 1) % 2]
                if f == 0:
                    acc = dot(patches(src, row), taps(l, 0, 2))
                    own_sum = acc[:, :chan].reshape(2, width, chan) + p0[l][pl.ds(2 * q, 2)]
                    p1[l][pl.ds(2 * q, 2)] += acc[:, chan:].reshape(2, width, chan)
                else:
                    acc = dot(patches(src, row), taps(l, 0, 1))
                    own_sum = acc.reshape(2, width, chan) + p1[l][pl.ds(2 * q, 2)]
                x = xs[pl.ds(row, 2)] + live_ref[l] * own_sum
                if l < depth - 1:
                    xs[pl.ds(row, 2)] = x
                    for k in range(2):
                        activate(dst, row + k, x[k])
                else:
                    outs[f, pl.ds(row - halo, 2)] = x.astype(jnp.bfloat16)
                return carry

            lax.fori_loop(0, (own + 2 * (halo - 1 - l)) // 2, layer, 0)

        @pl.when(jnp.logical_not(last))
        def _(f=f):
            x_copy(f, 1).start()

        both(jnp.logical_and(jnp.logical_not(last), has_down), [lambda f=f: x_copy(f, 0).start()])
        both(jnp.logical_and(jnp.logical_not(last), has_up), [lambda f=f: x_copy(f, 2).start()])
        pltpu.make_async_copy(outs.at[f], out.at[0, f], out_sem.at[f]).start()

    for f in range(frames):
        pltpu.make_async_copy(outs.at[f], out.at[0, f], out_sem.at[f]).wait()

        @pl.when(jnp.logical_not(last))
        def _(f=f):
            x_copy(f, 1).wait_send()

        both(jnp.logical_and(jnp.logical_not(last), has_down), [lambda f=f: x_copy(f, 0).wait_send()])
        both(jnp.logical_and(jnp.logical_not(last), has_up), [lambda f=f: x_copy(f, 2).wait_send()])
        both(seg0_down, [lambda f=f: clip_send(f, 0).wait_send()])
        both(seg0_up, [lambda f=f: clip_send(f, 2).wait_send()])
    for l in range(depth):
        both(has_down, [lambda l=l: cache_down(l).wait_send()])
        both(has_up, [lambda l=l: cache_up(l).wait_send()])


def per_device(clip, caches, weights, biases, section_layers):
    segments, bands = lax.axis_size("segment"), lax.axis_size("band")
    frames, own, width, chan = clip.shape
    depth = weights.shape[1]
    halo = depth
    ext = own + 2 * halo
    live = (jnp.arange(depth) < section_layers[0]).astype(jnp.float32)
    live = jnp.broadcast_to(live[:, None, None], (depth, 1, chan))
    bias = biases[0][:, None, :]
    bf, f32 = jnp.bfloat16, jnp.float32
    sums = [pltpu.VMEM((own + 2 * (halo - 1 - l), width, chan), f32) for l in range(depth)]
    dma = pltpu.SemaphoreType.DMA
    dims = (segments, bands, frames, own, width, chan, depth)
    return pl.pallas_call(
        functools.partial(kernel, dims),
        out_shape=jax.ShapeDtypeStruct((1,) + clip.shape, bf),
        in_specs=[pl.BlockSpec(memory_space=pltpu.VMEM)] * 2 + [pl.BlockSpec(memory_space=pl.ANY)] * 3,
        out_specs=pl.BlockSpec(memory_space=pl.ANY),
        scratch_shapes=[
            pltpu.VMEM((depth, 9, chan, 3 * chan), bf),
            pltpu.VMEM((depth, 2, ext, width, chan), bf),
            pltpu.VMEM((2, ext, width, 3 * chan), bf),
            pltpu.VMEM((2, ext, width, 3 * chan), bf),
            pltpu.VMEM((ext, width + 2 * PAD, chan), f32),
            pltpu.VMEM((ext, width, chan), f32),
            pltpu.VMEM((frames, ext, width, chan), bf),
            pltpu.VMEM((frames, own, width, chan), bf),
            *sums,
            *sums,
            dma((depth, 3)),
            dma((depth,)),
            dma((depth, 2)),
            dma((depth, 2)),
            dma,
            dma((frames, 2)),
            dma((frames, 3)),
            dma((frames, 3)),
            dma((frames,)),
        ],
        compiler_params=pltpu.CompilerParams(
            collective_id=0, has_side_effects=True, vmem_limit_bytes=56 * 2**20
        ),
    )(live, bias, clip, caches, weights)


def solution(mesh):
    placed = (
        P(None, "band", None, None),
        P("segment", None, None, "band", None, None),
        P("segment", None, None, None, None, None),
        P("segment", None, None),
        P("segment"),
    )
    return jax.shard_map(
        per_device,
        mesh=mesh,
        in_specs=placed,
        out_specs=P("segment", None, "band", None, None),
        check_vma=False,
    )
```

time: 742 us -> 106 us (0.14)
  the two profiles are of different devices: /device:TPU:102 before, /device:TPU:99 now
where the time goes in v1:
time: 106 us; the launch traced here: 105 us
  Pallas kernels  102 us (96%)
  local copies, waits for them, and re-layouts  2.37 us (2%)
    pallas_call x1, Pallas kernels, per_device(): pl.pallas_call(functools.partial(kernel, dims), out_shape=jax.ShapeDtypeS...  102 us

profile of v1, /device:TPU:99, one launch (start us, length us, event | category | flops | bytes accessed | tf_op | source)
XLA Modules:
  0.0 105.5 jit_solution(8629378125900835562)
XLA Ops:
  0.7 0.6 broadcast_in_dim.2.live_ref
  1.3 102.5 %shard_map.55 = bf16[1,2,4,160,128]{4,3,2,1,0:T(8,128)(2,1)} custom-call(f32[4,1,128]{2,1,0:T(1,128)} %broadcast_in_dim.2.live_ref, f32[4,1,128]{2,1,0:T(1,128)} %bitcast.3, bf16[2,4,160,128]{3,2,1,0:T(8,128)(2,1)} %clip.1, bf16[1,4,2,4,160,128]{5,4,3,2,1,0:T(8,128)(2,1)} %caches.1, bf16[1,4,9,3,128,128]{5,4,3,2,1,0:T(8,128)(2,1)} %weights.1), custom_call_target="tpu_custom_call" | custom-call | tf_op jit(solution)/shard_map/pallas_call | solution.py:269
  103.8 1.7 %copy.8 = bf16[1,2,4,160,128]{4,3,2,1,0:T(8,128)(2,1)} copy(bf16[1,2,4,160,128]{4,3,2,1,0:T(8,128)(2,1)} %shard_map.55) | data formatting | bytes 655360
  (1 shorter events, 0.0 us)

commit v2 on v0

v2 whole, which is shorter than its diff:
```python
import functools

import jax
import jax.numpy as jnp
from jax import lax
from jax.experimental import pallas as pl
from jax.experimental.pallas import tpu as pltpu
from jax.sharding import PartitionSpec as P

MESH = pl.DeviceIdType.MESH
CHUNK = 2
PARTS = 2


def kernel(dims, count_ref, bias_ref, clip, caches, weights, out, *scratch):
    segments, bands, frames, own, width, chan, depth = dims
    wp, cext, c3, xs, xin, outs = scratch[:6]
    a3 = scratch[6 : 6 + depth]
    sums = scratch[6 + depth : 6 + 2 * depth]
    (w_sem, cl_sem, ch_send, ch_recv, cm_sem, f_send, f_recv, z_send, z_recv, out_sem) = scratch[6 + 2 * depth :]
    halo = depth
    ext = own + 2 * halo
    taps = 3 * 3
    f32, bf16 = jnp.float32, jnp.bfloat16
    seg = lax.axis_index("segment")
    band = lax.axis_index("band")
    first, last = seg == 0, seg == segments - 1
    inner, sender = jnp.logical_not(first), jnp.logical_not(last)
    has_up, has_down = band > 0, band < bands - 1

    def when(cond, *steps):
        @pl.when(cond)
        def _():
            for step in steps:
                step()

    def w_copy(l, t, k):
        return pltpu.make_async_copy(
            weights.at[0, l, :, t],
            wp.at[l, t, pl.ds(3 * k, taps), :, pl.ds(k * chan, chan)],
            w_sem.at[l, t, k],
        )

    def own_cache(l):
        return pltpu.make_async_copy(caches.at[0, l], cext.at[l, :, pl.ds(halo, own)], cl_sem.at[l])

    clip_copy = pltpu.make_async_copy(clip, xin.at[:, pl.ds(halo, own)], cm_sem)
    for l in range(depth):
        own_cache(l).start()
        for t in range(3):
            for k in range(2):
                w_copy(l, t, k).start()
    when(first, clip_copy.start)

    barrier = pltpu.get_barrier_semaphore()

    def greet(cond, ds, db):
        @pl.when(cond)
        def _():
            pl.semaphore_signal(
                barrier, inc=1, device_id={"segment": seg + ds, "band": band + db}, device_id_type=MESH
            )
        return cond.astype(jnp.int32)

    greeted = greet(has_up, 0, -1) + greet(has_down, 0, 1) + greet(inner, -1, 0) + greet(sender, 1, 0)
    pl.semaphore_wait(barrier, greeted)

    def remote(src, dst, send, recv, ds, db):
        return pltpu.make_async_remote_copy(
            src, dst, send, recv, device_id={"segment": seg + ds, "band": band + db}, device_id_type=MESH
        )

    sides = ((0, 1, has_down, has_up), (1, -1, has_up, has_down))

    def cache_halo(l, side):
        src = pl.ds(l, own - l) if side == 0 else pl.ds(0, own - l)
        dst = pl.ds(l, own - l) if side == 0 else pl.ds(halo + own, own - l)
        return remote(
            caches.at[0, l, :, src], cext.at[l, :, dst], ch_send.at[l, side], ch_recv.at[l, side], 0, 1 - 2 * side
        )

    def forward(f, c, side, source):
        src = clip.at[f, pl.ds(CHUNK * c, CHUNK)] if source else xin.at[f, pl.ds(halo + CHUNK * c, CHUNK)]
        dst = xin.at[f, pl.ds(CHUNK * c + (halo + own) * side, CHUNK)]
        return remote(src, dst, f_send.at[f, c, side], f_recv.at[f, c, side], 0, 1 - 2 * side)

    def relay(f, c):
        return remote(
            outs.at[f, pl.ds(CHUNK * c, CHUNK)],
            xin.at[f, pl.ds(halo + CHUNK * c, CHUNK)],
            z_send.at[f, c],
            z_recv.at[f, c],
            1,
            0,
        )

    def send_clip(f):
        for side, _, to, _ in sides:
            when(jnp.logical_and(first, to), *[forward(f, c, side, True).start for c in range(PARTS)])

    for l in range(depth):
        for side, _, to, _ in sides:
            when(to, cache_halo(l, side).start)
        if l == depth - 2:
            send_clip(0)
    send_clip(1)

    def clear(l, carry):
        for t in range(3):
            wp[l, t, taps : taps + 3, :, 0:chan] = jnp.zeros((3, chan, chan), bf16)
            wp[l, t, 0:3, :, chan : 2 * chan] = jnp.zeros((3, chan, chan), bf16)
        return carry

    lax.fori_loop(0, depth, clear, 0)

    @pl.when(jnp.logical_not(has_up))
    def _():
        cext[:, :, 0:halo] = jnp.zeros((depth, 2, halo, width, chan), bf16)
        xin[:, 0:halo] = jnp.zeros((frames, halo, width, chan), bf16)

    @pl.when(jnp.logical_not(has_down))
    def _():
        cext[:, :, halo + own :] = jnp.zeros((depth, 2, halo, width, chan), bf16)
        xin[:, halo + own :] = jnp.zeros((frames, halo, width, chan), bf16)

    column = lax.broadcasted_iota(jnp.int32, (width, chan), 0)
    at_left, at_right = column == 0, column == width - 1

    def put_shifted(dst, row, value):
        left = jnp.where(at_left, 0.0, pltpu.roll(value, 1, 0))
        right = jnp.where(at_right, 0.0, pltpu.roll(value, width - 1, 0))
        dst[row, :, 0:chan] = left.astype(bf16)
        dst[row, :, chan : 2 * chan] = value.astype(bf16)
        dst[row, :, 2 * chan : 3 * chan] = right.astype(bf16)

    def pair_dot(l, t, sources):
        lhs = jnp.concatenate([src[row + i] for src, row in sources for i in range(4)], axis=1)
        rhs = wp[l, t : t + len(sources)].reshape(len(sources) * (taps + 3) * chan, 2 * chan)
        return jnp.dot(lhs, rhs, preferred_element_type=f32)

    for l in range(depth):
        own_cache(l).wait()
        for side, _, _, has in sides:
            when(has, cache_halo(l, side).wait_recv)
        for row in range(ext - 2 * l):
            for f in range(2):
                put_shifted(c3.at[l % 2, f], row, cext[l, f, l + row].astype(f32))
        for t in range(2):
            for k in range(2):
                w_copy(l, t, k).wait()
        bias = bias_ref[0, l : l + 1]
        older, newer = c3.at[l % 2, 0], c3.at[l % 2, 1]
        for row in range(0, own + 2 * (halo - 1 - l), 2):
            now = pair_dot(l, 0, [(older, row), (newer, row)])
            later = pair_dot(l, 0, [(newer, row)])
            for k in range(2):
                sums[l][0, row + k] = now[:, k * chan : (k + 1) * chan] + bias
                sums[l][1, row + k] = later[:, k * chan : (k + 1) * chan] + bias
    for l in range(depth):
        for k in range(2):
            w_copy(l, 2, k).wait()

    def activate(l, row, x):
        act = x * (0.5 * jnp.tanh(0.5 * x) + 0.5)
        if row < halo:
            act = jnp.where(has_up, act, 0.0)
        if row >= halo + own:
            act = jnp.where(has_down, act, 0.0)
        put_shifted(a3[l], row - l, act)

    lives = [jnp.clip(count_ref[0] - l, 0, 1).astype(f32) for l in range(depth)]

    def frame(f, carry):
        when(jnp.logical_and(first, f == 0), clip_copy.wait)
        for c in range(PARTS):
            when(inner, relay(f, c).wait_recv)
            for side, _, to, _ in sides:
                when(jnp.logical_and(inner, to), forward(f, c, side, False).start)

        def enter(row):
            x = xin[f, row].astype(f32)
            xs[row] = x
            activate(0, row, x)

        for row in range(halo, halo + own):
            enter(row)
        for side, _, _, has in sides:
            when(has, *[forward(f, c, side, False).wait_recv for c in range(PARTS)])
        for row in [*range(halo), *range(halo + own, ext)]:
            enter(row)
        for l in range(depth):
            for pair in range(0, own + 2 * (halo - 1 - l), 2):
                acc = pair_dot(l, 2, [(a3[l], pair)])
                for k in range(2):
                    row = l + 1 + pair + k
                    add = acc[:, k * chan : (k + 1) * chan] + sums[l][f, pair + k]
                    x = xs[row] + lives[l] * add
                    if l < depth - 1:
                        xs[row] = x
                        activate(l + 1, row, x)
                    else:
                        outs[f, row - halo] = x.astype(bf16)
                if l == depth - 1:
                    when(sender, relay(f, pair // 2).start)
        pltpu.make_async_copy(outs.at[f], out.at[0, f], out_sem.at[f]).start()

        @pl.when(f == 0)
        def _():
            for l in range(depth):
                for pair in range(0, own + 2 * (halo - 1 - l), 2):
                    acc = pair_dot(l, 1, [(a3[l], pair)])
                    for k in range(2):
                        sums[l][1, pair + k] += acc[:, k * chan : (k + 1) * chan]

        return carry

    lax.fori_loop(0, frames, frame, 0)

    for f in range(frames):
        pltpu.make_async_copy(outs.at[f], out.at[0, f], out_sem.at[f]).wait()
        for c in range(PARTS):
            when(sender, relay(f, c).wait_send)
            for side, _, to, _ in sides:
                when(to, forward(f, c, side, False).wait_send)
    for l in range(depth):
        for side, _, to, _ in sides:
            when(to, cache_halo(l, side).wait_send)


def per_device(clip, caches, weights, biases, section_layers):
    segments, bands = lax.axis_size("segment"), lax.axis_size("band")
    frames, own, width, chan = clip.shape
    depth = weights.shape[1]
    halo = depth
    ext = own + 2 * halo
    bf, f32 = jnp.bfloat16, jnp.float32
    dma = pltpu.SemaphoreType.DMA
    dims = (segments, bands, frames, own, width, chan, depth)
    return pl.pallas_call(
        functools.partial(kernel, dims),
        out_shape=jax.ShapeDtypeStruct((1,) + clip.shape, bf),
        in_specs=[pl.BlockSpec(memory_space=pltpu.SMEM), pl.BlockSpec(memory_space=pltpu.VMEM)]
        + [pl.BlockSpec(memory_space=pl.ANY)] * 3,
        out_specs=pl.BlockSpec(memory_space=pl.ANY),
        scratch_shapes=[
            pltpu.VMEM((depth, 3, 12, chan, 2 * chan), bf),
            pltpu.VMEM((depth, 2, ext, width, chan), bf),
            pltpu.VMEM((2, 2, ext, width, 3 * chan), bf),
            pltpu.VMEM((ext, width, chan), f32),
            pltpu.VMEM((frames, ext, width, chan), bf),
            pltpu.VMEM((frames, own, width, chan), bf),
            *[pltpu.VMEM((ext - 2 * l, width, 3 * chan), bf) for l in range(depth)],
            *[pltpu.VMEM((frames, ext - 2 * l - 2, width, chan), f32) for l in range(depth)],
            dma((depth, 3, 2)),
            dma((depth,)),
            dma((depth, 2)),
            dma((depth, 2)),
            dma,
            dma((frames, PARTS, 2)),
            dma((frames, PARTS, 2)),
            dma((frames, PARTS)),
            dma((frames, PARTS)),
            dma((frames,)),
        ],
        compiler_params=pltpu.CompilerParams(
            collective_id=0, has_side_effects=True, vmem_limit_bytes=56 * 2**20
        ),
    )(section_layers, biases, clip, caches, weights)


def solution(mesh):
    placed = (
        P(None, "band", None, None),
        P("segment", None, None, "band", None, None),
        P("segment", None, None, None, None, None),
        P("segment", None, None),
        P("segment"),
    )
    return jax.shard_map(
        per_device,
        mesh=mesh,
        in_specs=placed,
        out_specs=P("segment", None, "band", None, None),
        check_vma=False,
    )
```

time: 742 us -> 65.9 us (0.09); the launches traced: 727 us -> 65.7 us
  local copies, waits for them, and re-layouts: 414 us -> 1.72 us
  waiting for transfers between devices: 104 us -> 0 us
  starting transfers between devices: 95 us -> 0 us
  matrix products: 74.7 us -> 0 us
  Pallas kernels: 0 us -> 63.3 us
  other arithmetic: 24.5 us -> 0 us
  loops' own time: 15.4 us -> 0 us
    dot_general x20 -> x0, local copies, waits for them, and re-layouts: 225 us -> none  [conv_sum(): total = jnp.dot(patches, flat_kernel, preferred_element_type=jnp.float32)]
    another operation x40 -> x0, local copies, waits for them, and re-layouts: 130 us -> none  [conv_sum(): jnp.stack(pieces, axis=2).reshape(rows * width, 27 * padded.shape[-1])]
    ppermute x44 -> x0, waiting for transfers between devices: 104 us -> none  [the longest x20 81.1 us: extended(): lax.ppermute(tail, axis, [(i, (i + 1) % count) for i in range(ends)])]
    ppermute x44 -> x0, starting transfers between devices: 95 us -> none  [the longest x20 47.6 us: extended(): lax.ppermute(tail, axis, [(i, (i + 1) % count) for i in range(ends)])]
    dot_general x20 -> x0, matrix products: 74.7 us -> none  [conv_sum(): total = jnp.dot(patches, flat_kernel, preferred_element_type=jnp.float32)]
    pallas_call x0 -> x1, Pallas kernels: none -> 63.3 us  [per_device(): pl.pallas_call(functools.partial(kernel, dims), out_shape=jax.ShapeDtypeS...]
    dynamic_slice x20 -> x0, local copies, waits for them, and re-layouts: 24.6 us -> none  [layer_step(): kernel = lax.dynamic_index_in_dim(kernels, layer, 0, keepdims=False)]
    while x160 -> x0, local copies, waits for them, and re-layouts: 19 us -> none
  transfers between devices with their start and end apart: 44 -> 0, of which waited for: 24 -> 0; matrix products, arithmetic and copies ran while one was open for 5% -> 0% of each run, Pallas kernels for 0% -> 0%
where the time goes in v2:
time: 65.9 us; the launch traced here: 65.7 us
  Pallas kernels  63.3 us (96%)
  local copies, waits for them, and re-layouts  1.72 us (3%)
  between operations  0.66 us (1%)
    pallas_call x1, Pallas kernels, per_device(): pl.pallas_call(functools.partial(kernel, dims), out_shape=jax.ShapeDtypeS...  63.3 us
    unnamed x1, local copies, waits for them, and re-layouts  1.72 us

profile of v2, /device:TPU:102, one launch (start us, length us, event | category | flops | bytes accessed | tf_op | source)
XLA Modules:
  0.0 65.7 jit_solution(14152231725695001508)
XLA Ops:
  0.7 63.3 %shard_map.55 = bf16[1,2,4,160,128]{4,3,2,1,0:T(8,128)(2,1)} custom-call(s32[1]{0:T(128)S(6)} %copy.7.count_ref, f32[1,4,128]{2,1,0:T(4,128)} %bias_ref.1, bf16[2,4,160,128]{3,2,1,0:T(8,128)(2,1)} %clip.1, bf16[1,4,2,4,160,128]{5,4,3,2,1,0:T(8,128)(2,1)} %caches.1, bf16[1,4,9,3,128,128]{5,4,3,2,1,0:T(8,128)(2,1)} %weights.1), custom_call_target="tpu_custom_call" | custom-call | tf_op jit(solution)/shard_map/pallas_call | solution.py:239
  64.0 1.7 %copy.8 = bf16[1,2,4,160,128]{4,3,2,1,0:T(8,128)(2,1)} copy(bf16[1,2,4,160,128]{4,3,2,1,0:T(8,128)(2,1)} %shard_map.55) | data formatting | bytes 655360

commit v3 on v2

v3 whole, which is shorter than its diff:
```python
import functools

import jax
import jax.numpy as jnp
from jax import lax
from jax.experimental import pallas as pl
from jax.experimental.pallas import tpu as pltpu
from jax.sharding import PartitionSpec as P

MESH = pl.DeviceIdType.MESH
CHUNK = 1
PARTS = 4
HALF = 2


def kernel(dims, count_ref, bias_ref, clip, caches, weights, out, *scratch):
    segments, bands, frames, own, width, chan, depth = dims
    wp, cext, xin, mid, outs = scratch[:5]
    c3 = scratch[5 : 5 + depth]
    a3 = scratch[5 + depth : 6 + 2 * depth]
    sums = scratch[6 + 2 * depth : 6 + 3 * depth]
    xs = scratch[6 + 3 * depth : 7 + 4 * depth]
    (w_sem, cl_sem, ch_send, ch_recv, cm_sem, h_send, h_recv, f_send, f_recv, z_send, z_recv, out_sem) = scratch[7 + 4 * depth :]
    halo = depth
    ext = own + 2 * halo
    taps = 3 * 3
    f32, bf16 = jnp.float32, jnp.bfloat16
    seg = lax.axis_index("segment")
    band = lax.axis_index("band")
    first, last = seg == 0, seg == segments - 1
    inner, sender = jnp.logical_not(first), jnp.logical_not(last)
    odd = lax.rem(band, 2)
    has_up, has_down = band > 0, band < bands - 1
    has_far = jnp.logical_or(jnp.logical_and(odd == 0, has_up), jnp.logical_and(odd == 1, has_down))
    near, far = 0, 1
    below = (1 - odd, odd)

    def when(cond, *steps):
        @pl.when(cond)
        def _():
            for step in steps:
                step()

    def exists(side, *steps):
        if side == near:
            for step in steps:
                step()
        else:
            when(has_far, *steps)

    def edge(side, n):
        return below[side] * (own - n)

    def landing(side, n):
        return below[side] * (halo - n) + (1 - below[side]) * (halo + own)

    def region(side, n):
        return (1 - below[side]) * (halo - n) + below[side] * (halo + own)

    def w_copy(l, t, k):
        return pltpu.make_async_copy(
            weights.at[0, l, :, t],
            wp.at[l, t, pl.ds(3 * k, taps), :, pl.ds(k * chan, chan)],
            w_sem.at[l, t, k],
        )

    def own_cache(l):
        return pltpu.make_async_copy(caches.at[0, l], cext.at[l, :, pl.ds(halo, own)], cl_sem.at[l])

    clip_copy = pltpu.make_async_copy(clip, xin.at[:, pl.ds(halo, own)], cm_sem)

    def load(l):
        for t in range(2):
            for k in range(2):
                w_copy(l, t, k).start()

    for l in range(2):
        own_cache(l).start()
        load(l)

    barrier = pltpu.get_barrier_semaphore()

    def greet(cond, ds, db):
        @pl.when(cond)
        def _():
            pl.semaphore_signal(
                barrier, inc=1, device_id={"segment": seg + ds, "band": band + db}, device_id_type=MESH
            )
        return cond.astype(jnp.int32)

    greeted = greet(has_up, 0, -1) + greet(has_down, 0, 1) + greet(inner, -1, 0) + greet(sender, 1, 0)
    pl.semaphore_wait(barrier, greeted)
    for l in range(2, depth):
        own_cache(l).start()
        load(l)
    when(first, clip_copy.start)
    for l in range(depth):
        for k in range(2):
            w_copy(l, 2, k).start()

    def remote(src, dst, send, recv, ds, db):
        return pltpu.make_async_remote_copy(
            src, dst, send, recv, device_id={"segment": seg + ds, "band": band + db}, device_id_type=MESH
        )

    def beside(src, dst, send, recv, side):
        return remote(src, dst, send, recv, 0, 2 * below[side] - 1)

    def cache_halo(l, n, side, arrived=False):
        src = caches.at[0, l, :, pl.ds(edge(side, n), n)]
        dst = cext.at[l, :, pl.ds(region(side, n) if arrived else landing(side, n), n)]
        return beside(src, dst, ch_send.at[l, side], ch_recv.at[l, side], side)

    def clip_halo(f, side, arrived=False):
        src = clip.at[f, pl.ds(edge(side, HALF), HALF)]
        dst = xin.at[f, pl.ds(region(side, HALF) if arrived else landing(side, HALF), HALF)]
        return beside(src, dst, h_send.at[f, 0, side], h_recv.at[f, 0, side], side)

    def mid_halo(f, side, arrived=False):
        src = mid.at[f, pl.ds(halo + edge(side, HALF), HALF)]
        dst = mid.at[f, pl.ds(region(side, HALF) if arrived else landing(side, HALF), HALF)]
        return beside(src, dst, h_send.at[f, 1, side], h_recv.at[f, 1, side], side)

    def forward(f, c, side, arrived=False):
        src = xin.at[f, pl.ds(halo + CHUNK * c, CHUNK)]
        dst = xin.at[f, pl.ds((region(side, halo) if arrived else landing(side, halo)) + CHUNK * c, CHUNK)]
        return beside(src, dst, f_send.at[f, c, side], f_recv.at[f, c, side], side)

    def relay(f, c):
        return remote(
            outs.at[f, pl.ds(CHUNK * c, CHUNK)],
            xin.at[f, pl.ds(halo + CHUNK * c, CHUNK)],
            z_send.at[f, c],
            z_recv.at[f, c],
            1,
            0,
        )

    depths = tuple(own - l for l in range(depth))
    halves = tuple(HALF - l % HALF for l in range(depth))

    def start_first():
        for side in (far, near):
            exists(side, *[cache_halo(l, halves[l], side).start for l in range(HALF)], clip_halo(0, side).start)
            exists(side, *[cache_halo(l, halves[l], side).start for l in range(HALF, depth)])
        for side in (far, near):
            exists(side, clip_halo(1, side).start)

    def start_inner():
        for l in range(depth):
            for side in (far, near):
                exists(side, cache_halo(l, depths[l], side).start)

    when(first, start_first)
    when(inner, start_inner)

    def clear(l, carry):
        for t in range(3):
            wp[l, t, taps : taps + 3, :, 0:chan] = jnp.zeros((3, chan, chan), bf16)
            wp[l, t, 0:3, :, chan : 2 * chan] = jnp.zeros((3, chan, chan), bf16)
        return carry

    lax.fori_loop(0, depth, clear, 0)

    @pl.when(jnp.logical_not(has_far))
    def _():
        rows = pl.ds(region(far, halo), halo)
        for f in range(2):
            xin[f, rows] = jnp.zeros((halo, width, chan), bf16)
            mid[f, rows] = jnp.zeros((halo, width, chan), bf16)
            for l in range(depth):
                cext[l, f, rows] = jnp.zeros((halo, width, chan), bf16)

    column = lax.broadcasted_iota(jnp.int32, (width, chan), 0)
    at_left, at_right = column == 0, column == width - 1

    def put_shifted(dst, row, value):
        left = jnp.where(at_left, 0.0, pltpu.roll(value, 1, 0))
        right = jnp.where(at_right, 0.0, pltpu.roll(value, width - 1, 0))
        dst[row, :, 0:chan] = left.astype(bf16)
        dst[row, :, chan : 2 * chan] = value.astype(bf16)
        dst[row, :, 2 * chan : 3 * chan] = right.astype(bf16)

    def pair_dot(l, t, sources, row):
        lhs = jnp.concatenate([src[row - 1 + i] for src in sources for i in range(4)], axis=1)
        rhs = wp[l, t : t + len(sources)].reshape(len(sources) * (taps + 3) * chan, 2 * chan)
        return jnp.dot(lhs, rhs, preferred_element_type=f32)

    def spread(l, start, n):
        def step(i, carry):
            for f in range(2):
                put_shifted(c3[l].at[f], start + i, cext[l, f, start + i].astype(f32))
            return carry

        lax.fori_loop(0, n, step, 0)

    def history(l, rows):
        bias = bias_ref[0, l : l + 1]
        older, newer = c3[l].at[0], c3[l].at[1]
        for row in rows:
            now = pair_dot(l, 0, [older, newer], row)
            later = pair_dot(l, 0, [newer], row)
            for k in range(2):
                sums[l][0, row + k] = now[:, k * chan : (k + 1) * chan] + bias
                sums[l][1, row + k] = later[:, k * chan : (k + 1) * chan] + bias

    def renew(l, rows):
        for row in rows:
            acc = pair_dot(l, 1, [acts(l, 0)], row)
            for k in range(2):
                sums[l][1, row + k] += acc[:, k * chan : (k + 1) * chan]

    def at(l, f):
        return depth if l == HALF and isinstance(f, int) and f == 1 else l

    def acts(l, f):
        return a3[at(l, f)]

    def activate(l, f, row, x, outside=None):
        act = x * (0.5 * jnp.tanh(0.5 * x) + 0.5)
        if outside is None:
            line = band * own + row - halo
            act = jnp.where(jnp.logical_and(line >= 0, line < bands * own), act, 0.0)
        elif outside:
            act = jnp.where(has_far, act, 0.0)
        put_shifted(acts(l, f), row, act)

    def far_row(parity, row):
        if parity is None:
            return None
        return row < halo if parity == 0 else row >= halo + own

    def enter(src, f, l, rows, parity=None):
        for row in rows:
            x = src[f, row].astype(f32)
            xs[at(l, f)][row] = x
            activate(l, f, row, x, far_row(parity, row))

    lives = [jnp.clip(count_ref[0] - l, 0, 1).astype(f32) for l in range(depth)]

    def layer(f, l, rows, keep=False, parity=None):
        for row in rows:
            acc = pair_dot(l, 2, [acts(l, f)], row)
            for k in range(2):
                add = acc[:, k * chan : (k + 1) * chan] + sums[l][f, row + k]
                x = xs[at(l, f)][row + k] + lives[l] * add
                if l < depth - 1:
                    xs[at(l + 1, f)][row + k] = x
                    activate(l + 1, f, row + k, x, far_row(parity, row + k))
                    if keep:
                        mid[f, row + k] = x.astype(bf16)
                else:
                    outs[f, row + k - halo] = x.astype(bf16)

    def finish(f):
        for c in range(PARTS):
            if CHUNK * c % 2 == 0:
                layer(f, depth - 1, [halo + CHUNK * c])
            if CHUNK * c % 2 or CHUNK > 1:
                for part in range(c - (CHUNK == 1), c + 1):
                    when(sender, relay(f, part).start)
        pltpu.make_async_copy(outs.at[f], out.at[0, f], out_sem.at[f]).start()

    def load_taps(l, times):
        for t in times:
            for k in range(2):
                w_copy(l, t, k).wait()

    middle = list(range(halo, halo + own))

    def beyond(side, n):
        return [region(side, n) + i for i in range(n)]

    def first_section(parity):
        odd = parity

        def beyond(side, n):
            at_top = (parity, 1 - parity)[side]
            return [(halo - n if at_top else halo + own) + i for i in range(n)]

        early = ([5 - 2 * odd, 7 - 2 * odd], [6 - 2 * odd])
        late = ([3 + 4 * odd], [4 + 2 * odd])
        both = ([3, 5, 7], [4, 6])
        for l in range(depth):
            own_cache(l).wait()
            cache_halo(l, halves[l], near, True).wait_recv()
            spread(l, halo, own)
            spread(l, beyond(near, halves[l])[0], halves[l])
            load_taps(l, (0, 1))
            history(l, early[l % HALF])
        clip_copy.wait()
        load_taps(0, (2,))

        def more(l):
            when(has_far, cache_halo(l, halves[l], far, True).wait_recv)
            spread(l, beyond(far, halves[l])[0], halves[l])
            history(l, late[l % HALF])
            if l > 0:
                load_taps(l, (2,))

        for stage in range(2):
            for f in range(frames):
                src, arrival = ((xin, clip_halo), (mid, mid_halo))[stage]
                l0, l1 = 2 * stage, 2 * stage + 1
                if f == 1:
                    renew(l0, both[0])
                    renew(l1, both[1])
                if stage == 0:
                    enter(src, f, l0, middle, parity)
                arrival(f, near, True).wait_recv()
                enter(src, f, l0, beyond(near, HALF), parity)
                layer(f, l0, early[0], parity=parity)
                if f == 0 and stage == 0:
                    more(l0)
                    more(l1)
                when(has_far, arrival(f, far, True).wait_recv)
                enter(src, f, l0, beyond(far, HALF), parity)
                layer(f, l0, late[0], parity=parity)
                if stage == 0:
                    layer(f, l1, both[1], True, parity)
                    for side in (far, near):
                        exists(side, mid_halo(f, side).start)
                else:
                    finish(f)
            if stage == 0:
                more(2)
                more(3)

    def inner_section():
        for l in range(depth):
            own_cache(l).wait()
            cache_halo(l, depths[l], near, True).wait_recv()
            when(has_far, cache_halo(l, depths[l], far, True).wait_recv)
            spread(l, l, ext - 2 * l)
            load_taps(l, (0, 1))
            history(l, range(l + 1, ext - 1 - l, 2))
        for l in range(depth):
            load_taps(l, (2,))

        def take(f):
            for c in range(PARTS):
                relay(f, c).wait_recv()
                for side in (far, near):
                    exists(side, forward(f, c, side).start)

        take(0)

        def rows_of(parity, f):
            outer = list(range(halo)), list(range(halo + own, ext))
            near_rows, far_rows = outer[1 - parity], outer[parity]
            first_rows = ([5, 7, 9], [6, 8], [7]), ([1, 3, 5], [2, 4], [3])
            last_rows = ([1, 3], [2, 4], [3, 5]), ([7, 9], [6, 8], [5, 7])
            enter(xin, f, 0, middle, parity)
            for c in range(PARTS):
                forward(f, c, near, True).wait_recv()
            enter(xin, f, 0, near_rows, parity)
            for l in range(depth - 1):
                layer(f, l, first_rows[parity][l], parity=parity)
            when(has_far, *[forward(f, c, far, True).wait_recv for c in range(PARTS)])
            enter(xin, f, 0, far_rows, parity)
            for l in range(depth - 1):
                layer(f, l, last_rows[parity][l], parity=parity)
            finish(f)

        def frame(f, carry):
            for parity in range(2):
                when(odd == parity, lambda parity=parity: rows_of(parity, f))

            @pl.when(f == 0)
            def _():
                take(1)
                for l in range(depth):
                    renew(l, range(l + 1, ext - 1 - l, 2))

            return carry

        lax.fori_loop(0, frames, frame, 0)
        for f in range(frames):
            for c in range(PARTS):
                for side in (far, near):
                    exists(side, forward(f, c, side).wait_send)
        for l in range(depth):
            for side in (far, near):
                exists(side, cache_halo(l, depths[l], side).wait_send)

    def end_first():
        for f in range(frames):
            for side in (far, near):
                exists(side, clip_halo(f, side).wait_send, mid_halo(f, side).wait_send)
        for l in range(depth):
            for side in (far, near):
                exists(side, cache_halo(l, halves[l], side).wait_send)

    for parity in range(2):
        when(jnp.logical_and(first, odd == parity), lambda parity=parity: first_section(parity))
    when(first, end_first)
    when(inner, inner_section)

    for f in range(frames):
        pltpu.make_async_copy(outs.at[f], out.at[0, f], out_sem.at[f]).wait()
        for c in range(PARTS):
            when(sender, relay(f, c).wait_send)


def per_device(clip, caches, weights, biases, section_layers):
    segments, bands = lax.axis_size("segment"), lax.axis_size("band")
    frames, own, width, chan = clip.shape
    depth = weights.shape[1]
    halo = depth
    ext = own + 2 * halo
    bf, f32 = jnp.bfloat16, jnp.float32
    dma = pltpu.SemaphoreType.DMA
    dims = (segments, bands, frames, own, width, chan, depth)
    return pl.pallas_call(
        functools.partial(kernel, dims),
        out_shape=jax.ShapeDtypeStruct((1,) + clip.shape, bf),
        in_specs=[pl.BlockSpec(memory_space=pltpu.SMEM), pl.BlockSpec(memory_space=pltpu.VMEM)]
        + [pl.BlockSpec(memory_space=pl.ANY)] * 3,
        out_specs=pl.BlockSpec(memory_space=pl.ANY),
        scratch_shapes=[
            pltpu.VMEM((depth, 3, 12, chan, 2 * chan), bf),
            pltpu.VMEM((depth, 2, ext, width, chan), bf),
            pltpu.VMEM((frames, ext, width, chan), bf),
            pltpu.VMEM((frames, ext, width, chan), bf),
            pltpu.VMEM((frames, own, width, chan), bf),
            *[pltpu.VMEM((2, ext, width, 3 * chan), bf)] * depth,
            *[pltpu.VMEM((ext, width, 3 * chan), bf)] * (depth + 1),
            *[pltpu.VMEM((frames, ext, width, chan), f32)] * depth,
            *[pltpu.VMEM((ext, width, chan), f32)] * (depth + 1),
            dma((depth, 3, 2)),
            dma((depth,)),
            dma((depth, 2)),
            dma((depth, 2)),
            dma,
            dma((frames, 2, 2)),
            dma((frames, 2, 2)),
            dma((frames, PARTS, 2)),
            dma((frames, PARTS, 2)),
            dma((frames, PARTS)),
            dma((frames, PARTS)),
            dma((frames,)),
        ],
        compiler_params=pltpu.CompilerParams(
            collective_id=0, has_side_effects=True, vmem_limit_bytes=56 * 2**20
        ),
    )(section_layers, biases, clip, caches, weights)


def solution(mesh):
    placed = (
        P(None, "band", None, None),
        P("segment", None, None, "band", None, None),
        P("segment", None, None, None, None, None),
        P("segment", None, None),
        P("segment"),
    )
    return jax.shard_map(
        per_device,
        mesh=mesh,
        in_specs=placed,
        out_specs=P("segment", None, "band", None, None),
        check_vma=False,
    )
```

time: 65.9 us -> 58.3 us (0.88)
  Pallas kernels: 63.3 us -> 55.7 us
    pallas_call x1, Pallas kernels: 63.3 us -> 55.7 us  [per_device(): pl.pallas_call(functools.partial(kernel, dims), out_shape=jax.ShapeDtypeS...]
where the time goes in v3:
time: 58.3 us; the launch traced here: 58.1 us
  Pallas kernels  55.7 us (96%)
  local copies, waits for them, and re-layouts  1.72 us (3%)
  between operations  0.66 us (1%)
    pallas_call x1, Pallas kernels, per_device(): pl.pallas_call(functools.partial(kernel, dims), out_shape=jax.ShapeDtypeS...  55.7 us
    unnamed x1, local copies, waits for them, and re-layouts  1.72 us

profile of v3, /device:TPU:102, one launch (start us, length us, event | category | flops | bytes accessed | tf_op | source)
XLA Modules:
  0.0 58.1 jit_solution(7216696932587229832)
XLA Ops:
  0.7 55.7 %shard_map.55 = bf16[1,2,4,160,128]{4,3,2,1,0:T(8,128)(2,1)} custom-call(s32[1]{0:T(128)S(6)} %copy.7.count_ref, f32[1,4,128]{2,1,0:T(4,128)} %bias_ref.1, bf16[2,4,160,128]{3,2,1,0:T(8,128)(2,1)} %clip.1, bf16[1,4,2,4,160,128]{5,4,3,2,1,0:T(8,128)(2,1)} %caches.1, bf16[1,4,9,3,128,128]{5,4,3,2,1,0:T(8,128)(2,1)} %weights.1), custom_call_target="tpu_custom_call" | custom-call | tf_op jit(solution)/shard_map/pallas_call | solution.py:414
  56.4 1.7 %copy.8 = bf16[1,2,4,160,128]{4,3,2,1,0:T(8,128)(2,1)} copy(bf16[1,2,4,160,128]{4,3,2,1,0:T(8,128)(2,1)} %shard_map.55) | data formatting | bytes 655360
